TPU v7x, 256 devices: a whole 4x4x8 slice. The times are simulated.
256 devices in a mesh: band: 8 (over x, core), grid: 32 (over z, y).
Axes of the slice: x: 4, y: 4, z: 8, core: 2. Of those that a mesh axis runs over, the one named last changes fastest.
Arguments:
- coeffs: float32 [2, 8, 22016, 128], P(None, 'band', 'grid'), may hold values from -6 to 6
- stick_ids: int32 [22016], replicated, may hold values from -1 to 16383, as said below
- band_weights: float32 [8], P('band'), may hold values from 0.02 to 0.2
- aug_functions: float32 [128, 16, 256], replicated, may hold values from -0.1875 to 0.1875
- atom_offsets: int32 [64, 3], replicated, may hold values from 0 to 255, as said below
- intersection_list: int32 [32, 7], P('grid'), may hold values from 0 to 63, as said below
- atom_slots: int32 [128], replicated, may hold values from -1 to 63, as said below
Outputs:
- density: float32 [256, 256, 256], P('grid', 'band')
- atom_totals: float32 [128, 128, 128], P('grid')
Inputs may be any that keep to these rules, and one draw needn't show every extreme that they name: `stick_ids`: every column of the 128 x 128 wave-vector columns stands in exactly one slot; empty slots hold -1; some index of grid has all its 688 slots filled. `atom_slots`: every atom stands in exactly one slot; empty slots hold -1; some index of grid has all its 4 slots filled. `atom_offsets`: columns are x0, y0, z0; atom a has z0 in a * 4 .. (a + 1) * 4 - 1. `intersection_list`: row d names 7 distinct atoms, among them every atom whose box has a layer on the planes of index d of grid.
All inputs are finite; a program needn't handle non-finite values.
Results may differ from a plain program's by a relative error of at most 0.0003.
Values sent between devices are 32-bit elements; how exact they have to be, the bound alone decides.
A program may use at most 192 MiB of HBM per device.

v0:
```python
import jax
import jax.numpy as jnp
from jax import lax
from jax.sharding import PartitionSpec as P

GRID = 256
KG = 128
BOX = 16
NFUNC = 128


HIGH = lax.Precision.HIGHEST


def dft_tables(amount, length):
    frequency = jnp.arange(amount, dtype=jnp.int32) - amount // 2
    points = jnp.arange(length, dtype=jnp.int32)
    phases = frequency[:, None] * points[None, :] % length
    angles = phases.astype(jnp.float32) * (2.0 * jnp.pi / length)
    factor = amount ** (-0.5)
    return (jnp.cos(angles) * factor, jnp.sin(angles) * factor)


def complex_apply(form, real_part, imag_part, cosine, sine):
    real_out = jnp.einsum(form, real_part, cosine, precision=HIGH) - jnp.einsum(
        form, imag_part, sine, precision=HIGH
    )
    imag_out = jnp.einsum(form, real_part, sine, precision=HIGH) + jnp.einsum(
        form, imag_part, cosine, precision=HIGH
    )
    return (real_out, imag_out)


def column_slots(stick_ids):
    total = KG * KG
    target = jnp.where(stick_ids >= 0, stick_ids, total)
    filled = (
        jnp.zeros((total + 1,), jnp.int32)
        .at[target]
        .set(jnp.arange(stick_ids.shape[0], dtype=jnp.int32))
    )
    return filled[:total]


def layer_pick(first, lowest, layers, planes):
    planes_here = first + jnp.arange(planes, dtype=jnp.int32)
    depth = (planes_here - lowest) % GRID
    return (depth[:, None] == layers[None, :]).astype(jnp.float32)


def wrap_pad(field):
    field = jnp.concatenate([field, field[..., :BOX, :]], axis=-2)
    return jnp.concatenate([field, field[..., :BOX]], axis=-1)


def fold_pad(padded):
    rows = padded[:, :GRID, :] + jnp.pad(padded[:, GRID:, :], ((0, 0), (0, GRID - BOX), (0, 0)))
    return rows[:, :, :GRID] + jnp.pad(rows[:, :, GRID:], ((0, 0), (0, 0), (0, GRID - BOX)))


def on_device(
    coeffs, stick_ids, band_weights, aug_functions, atom_offsets, intersection_list, atom_slots
):
    planes = GRID // lax.axis_size("grid")
    first_plane = lax.axis_index("grid") * planes
    listed = intersection_list[0]
    listed_offsets = atom_offsets[listed]
    listed_count = listed.shape[0]
    own_rows = atom_slots.shape[0] // lax.axis_size("grid")
    every_layer = jnp.arange(BOX, dtype=jnp.int32)
    cosine, sine = dft_tables(KG, GRID)
    slot_map = column_slots(stick_ids)
    z_real, z_imag = complex_apply("bsg,gn->bns", coeffs[0], coeffs[1], cosine, sine)
    sticks = jnp.stack([z_real, z_imag])

    def project_atom(padded_wave, offsets):
        bands_here = padded_wave.shape[1]
        pick = layer_pick(first_plane, offsets[2], every_layer, planes)
        chosen = jnp.einsum("pk,ikc->ipc", pick, aug_functions, precision=HIGH)
        window = lax.dynamic_slice(
            padded_wave, (0, 0, 0, offsets[0], offsets[1]), (2, bands_here, planes, BOX, BOX)
        )
        window = window.reshape(2, bands_here, planes, BOX * BOX)
        return jnp.einsum("ipc,xbpc->bxi", chosen, window, precision=HIGH)

    received = lax.all_to_all(sticks, "grid", split_axis=2, concat_axis=3, tiled=True)
    bands_here = received.shape[1]
    spectra = received[:, :, :, slot_map].reshape(2, bands_here, planes, KG, KG)
    y_real, y_imag = complex_apply("bpxy,yn->bpxn", spectra[0], spectra[1], cosine, sine)
    x_real, x_imag = complex_apply("bpxn,xm->bpmn", y_real, y_imag, cosine, sine)
    band_density = x_real * x_real + x_imag * x_imag
    padded_wave = wrap_pad(jnp.stack([x_real, x_imag]))
    found = jax.vmap(lambda offsets: project_atom(padded_wave, offsets), out_axes=1)(listed_offsets)
    density = jnp.einsum("b,bpxy->pxy", band_weights, band_density, precision=HIGH)
    flat_found = jnp.transpose(found, (1, 0, 2, 3)).reshape(listed_count, -1)
    pick = (atom_slots[:, None] == listed[None, :]).astype(jnp.float32)
    owned = lax.psum_scatter(
        jnp.dot(pick, flat_found, precision=HIGH), "grid", scatter_dimension=0, tiled=True
    )
    owned = owned.reshape(own_rows, band_weights.shape[0], 2, NFUNC)
    partial_matrices = jnp.einsum("b,sbxi,sbxj->sij", band_weights, owned, owned, precision=HIGH)
    atom_totals = lax.psum(partial_matrices, "band")
    slot_pick = (listed[:, None] == atom_slots[None, :]).astype(jnp.float32)
    thickness = BOX // lax.axis_size("band")
    band_layers = lax.axis_index("band") * thickness + jnp.arange(thickness, dtype=jnp.int32)
    layers_here = lax.dynamic_slice_in_dim(
        aug_functions, lax.axis_index("band") * thickness, thickness, 1
    )
    layers_here = layers_here.reshape(NFUNC, thickness * BOX * BOX)
    halfway = jnp.einsum("sij,jc->sic", atom_totals, layers_here, precision=HIGH)
    box_part = jnp.sum(halfway * layers_here[None], axis=1)
    every_box = lax.all_gather(box_part, "grid", axis=0, tiled=True)
    mine = jnp.dot(slot_pick, every_box, precision=HIGH).reshape(listed_count, thickness, BOX * BOX)

    def box_piece(offsets, box_rows):
        pick = layer_pick(first_plane, offsets[2], band_layers, planes)
        return jnp.dot(pick, box_rows, precision=HIGH).reshape(planes, BOX, BOX)

    pieces = jax.vmap(box_piece)(listed_offsets, mine)

    def place(index, acc):
        corner = (0, listed_offsets[index, 0], listed_offsets[index, 1])
        current = lax.dynamic_slice(acc, corner, (planes, BOX, BOX))
        return lax.dynamic_update_slice(acc, current + pieces[index], corner)

    padded = lax.fori_loop(
        0, listed_count, place, jnp.zeros((planes, GRID + BOX, GRID + BOX), jnp.float32)
    )
    total = density + fold_pad(padded)
    result = lax.psum_scatter(total, "band", scatter_dimension=1, tiled=True)
    return (result, atom_totals)


def solution(mesh):
    placed = (P(None, "band", "grid", None), P(), P("band"), P(), P(), P("grid", None), P())
    return jax.shard_map(
        on_device,
        mesh=mesh,
        in_specs=placed,
        out_specs=(P("grid", "band", None), P("grid", None, None)),
        check_vma=False,
    )
```

profile of v0, /device:TPU:1, one launch (start us, length us, event | category | flops | bytes accessed | tf_op | source)
XLA Modules:
  0.0 785.0 jit_solution(15550919658142856036)
XLA Ops:
  18.4 12.3 %all-to-all-start = ((f32[2,1,256,688]{3,1,0,2:T(1,128)}), f32[2,1,256,688]{3,1,0,2:T(1,128)}, u32[]{:S(2)}, u32[]{:S(2)}) async-start(f32[2,1,256,688]{3,1,0,2:T(1,128)} %copy.39), calls=%async_computation | async-start | bytes 3145728 | tf_op jit(solution)/shard_map/all_to_all | solution.py:86
  31.7 81.4 %scatter_custom_fusion = s32[16385]{0:T(1024)S(1)} fusion(s32[22016]{0:T(1024)S(1)} %compare_select_fusion, s32[22016]{0:T(1024)S(1)} %iota.50, s32[]{:T(128)} %constant.80.clone.1), kind=kCustom, calls=%fused_computation.75 | custom fusion | bytes 65544 | tf_op jit(solution)/shard_map/scatter | solution.py:40
  113.4 5.2 convolution_bitcast_fusion
  121.2 21.8 %copy.67 = f32[2,1,8,32,688]{2,0,4,3,1:T(2,128)} copy(f32[2,1,8,32,688]{4,2,3,0,1:T(8,128)} %bitcast.131) | data formatting | bytes 2818048 | tf_op jit(solution)/shard_map/all_to_all | solution.py:86
  143.0 118.9 %gather_fusion = f32[16384,2,8]{2,1,0:T(2,128)} fusion(f32[2,8,22016]{1,0,2:T(2,128)} %bitcast.129, s32[16384]{0:T(1024)S(1)} %fusion.42), kind=kCustom, calls=%fused_computation | custom fusion | bytes 2162688 | tf_op jit(solution)/shard_map/gather | solution.py:88
  262.0 19.3 %fusion.133 = (f32[1,8,16384]{1,0,2:T(1,128)}, f32[1,8,16384]{1,0,2:T(1,128)}) fusion(f32[2,8,16384]{1,0,2:T(2,128)} %bitcast.130), kind=kLoop, calls=%fused_computation.178 | loop fusion | bytes 2097152 | tf_op jit(solution)/shard_map/slice | solution.py:89
  281.3 5.1 copy.68
  291.4 5.3 copy.70
  311.5 3.0 fusion.2
  314.5 75.1 %copy.53 = f32[2,1,8,272,272]{2,0,1,4,3:T(2,128)} copy(f32[2,1,8,272,272]{4,3,2,1,0:T(8,128)} %fusion.2) | data formatting | bytes 9469952 | tf_op jit(solution)/shard_map/concatenate | solution.py:53
  389.6 5.3 gather_fusion.2
  397.6 9.8 %fusion.11 = f32[1,7,2,128]{3,2,1,0:T(2,128)S(1)} fusion(f32[7,2,8,256]{3,1,2,0:T(2,128)S(1)} %copy.54, f32[7,128,8,256]{3,2,1,0:T(8,128)} %convolution_bitcast_fusion), kind=kOutput, calls=%fused_computation.34 | convolution fusion | flops 44040192 | bytes 7461888 | tf_op jit(solution)/shard_map/vmap(ipc,xbpc->bxi)/dot_general | solution.py:84
  410.3 137.9 %all-reduce.8.cloned.1.call-done = f32[128,256]{1,0:T(8,128)} async-done(((f32[128,256]{1,0:T(8,128)}), f32[128,256]{1,0:T(8,128)}) %all-reduce.8.cloned.1.call-update) | async-done | bytes 131088
  550.8 66.1 %all-reduce.6.cloned.1.call-done = f32[4,128,128]{2,1,0:T(8,128)} async-done(((f32[4,128,128]{2,1,0:T(8,128)}), f32[4,128,128]{2,1,0:T(8,128)}) %all-reduce.6.cloned.1.call-update) | async-done | bytes 262160 | tf_op jit(solution)/shard_map/psum | solution.py:102
  618.9 38.3 %all-gather = f32[32,4,512]{2,1,0:T(4,128)S(1)} all-gather(f32[1,4,512]{2,1,0:T(4,128)S(1)} %bitcast.135), channel_id=1, replica_groups=mesh['band'=8,'grid'=32] {'grid'}, dimensions={0}, use_global_device_ids=true | all-gather | bytes 270336 | tf_op jit(solution)/shard_map/all_gather | solution.py:112
  659.9 67.9 %while.13 = (s32[]{:T(128)}, f32[8,272,272]{2,1,0:T(8,128)}, s32[7,3]{0,1:T(4,128)S(1)}, f32[7,8,16,16]{3,2,1,0:T(8,128)S(1)}, s32[]{:T(128)}, /*index=5*/s32[]{:T(128)}, s32[]{:T(128)}) while((s32[]{:T(128)}, f32[8,272,272]{2,1,0:T(8,128)}, s32[7,3]{0,1:T(4,128)S(1)}, f32[7,8,16,16]{3,2,1,0:T(8,128)S(1)}, s32[]{:T(128)}, ...), condition=%wide.region_5.6_spmd, body=%wide.region_4.5_spmd.sunk | while | flops 2056 | bytes 41141 | solution.py:126
  665.3 4.3 dynamic_update_slice.8
  675.0 4.3 dynamic_update_slice.8
  684.7 4.3 dynamic_update_slice.8
  694.4 4.3 dynamic_update_slice.8
  704.1 4.3 dynamic_update_slice.8
  713.8 4.3 dynamic_update_slice.8
  723.5 4.3 dynamic_update_slice.8
  733.7 43.9 %reduce-scatter.2.cloned.1.call-done = f32[8,32,256]{2,1,0:T(8,128)} async-done(((f32[8,256,256]{2,1,0:T(8,128)}), f32[8,32,256]{2,1,0:T(8,128)}) %reduce-scatter.2.cloned.1.call-update) | async-done | bytes 262160 | tf_op jit(solution)/shard_map/reduce_scatter | solution.py:130
  (98 shorter events, 64.2 us)
Async XLA Ops:
  7.2 106.2 %copy-start = (f32[128,16,256]{2,1,0:T(8,128)S(1)}, f32[128,16,256]{2,1,0:T(8,128)}, u32[]{:S(2)}) copy-start(f32[128,16,256]{2,1,0:T(8,128)} %param.12) | copy-start | bytes 6291460
  7.2 6.8 copy-start.6
  15.4 15.3 %copy-start.11 = (s32[64,3]{0,1:T(4,128)S(1)}, s32[64,3]{0,1:T(4,128)}, u32[]{:S(2)}) copy-start(s32[64,3]{0,1:T(4,128)} %param.13) | copy-start | bytes 2308
  15.4 15.4 %copy-start.9 = (s32[1,7]{1,0:T(1,128)S(1)}, s32[1,7]{1,0:T(1,128)}, u32[]{:S(2)}) copy-start(s32[1,7]{1,0:T(1,128)} %param.14) | copy-start | bytes 88
  18.4 13.2 %copy-start.8 = (s32[22016]{0:T(1024)S(1)}, s32[22016]{0:T(1024)}, u32[]{:S(2)}) copy-start(s32[22016]{0:T(1024)} %param.10) | copy-start | bytes 264196
  18.4 100.2 %all-to-all-start = ((f32[2,1,256,688]{3,1,0,2:T(1,128)}), f32[2,1,256,688]{3,1,0,2:T(1,128)}, u32[]{:S(2)}, u32[]{:S(2)}) async-start(f32[2,1,256,688]{3,1,0,2:T(1,128)} %copy.39), calls=%async_computation | async-start | bytes 3145728 | tf_op jit(solution)/shard_map/all_to_all | solution.py:86
  30.7 517.5 %all-reduce.8.cloned.1.call-start = ((), (), s32[]{:S(2)}) async-start(), calls=%async_computation.4 | async-start | bytes 262144
  299.5 4.6 copy-start.5
  307.9 2.4 copy-start.1
  310.2 1.3 copy-start.3
  397.6 9.8 %copy-start.10 = (s32[128]{0:T(128)S(1)}, s32[128]{0:T(128)}, u32[]{:S(2)}) copy-start(s32[128]{0:T(128)} %param.15) | copy-start | bytes 1540
  397.6 11.4 %copy-start.12 = (u32[256]{0:T(256)S(1)}, u32[256]{0:T(256)}, u32[]{:S(2)}) copy-start(u32[256]{0:T(256)} %constant.145) | copy-start | bytes 3076
  408.3 208.6 %all-reduce.6.cloned.1.call-start = ((), (), s32[]{:S(2)}) async-start(), calls=%async_computation.2 | async-start | bytes 524288 | tf_op jit(solution)/shard_map/psum | solution.py:102
  550.2 227.4 %reduce-scatter.2.cloned.1.call-start = ((), (), s32[]{:S(2)}) async-start(), calls=%async_computation.3 | async-start | bytes 2359296 | tf_op jit(solution)/shard_map/reduce_scatter | solution.py:130
  728.8 2.5 copy-start.2
  728.8 3.2 copy-start.4
  731.9 45.6 %copy-start.7 = (f32[4,128,128]{2,1,0:T(8,128)S(1)}, f32[4,128,128]{2,1,0:T(8,128)}, u32[]{:S(2)}) copy-start(f32[4,128,128]{2,1,0:T(8,128)} %all-reduce.6.cloned.1.call-done) | copy-start | bytes 786436
Sparse Core Ops, SparseCore 0:
  408.4 139.6 all-reduce.7
  551.0 65.8 all-reduce.5
  733.8 43.6 reduce-scatter.1
where the time goes:
time: 800 us; the launch traced here: 785 us
  local copies, waits for them, and re-layouts  383 us (48%)
  waiting for transfers between devices  248 us (31%)
  matrix products  46 us (6%)
  blocking collectives  38.3 us (5%)
  loops' own time  26.6 us (3%)
  between operations  15.7 us (2%)
  other arithmetic  14.8 us (2%)
  starting transfers between devices  12.4 us (2%)
    unnamed x4, waiting for transfers between devices  138 us
    gather x1, local copies, waits for them, and re-layouts, on_device(): spectra = received[:, :, :, slot_map].reshape(2, bands_here, planes, KG, KG)  119 us
    scatter x1, local copies, waits for them, and re-layouts, column_slots(): filled = jnp.zeros((total + 1,), jnp.int32).at[target].set(jnp.arange(sti...  81.4 us
    concatenate x1, local copies, waits for them, and re-layouts, wrap_pad(): return jnp.concatenate([field, field[..., :BOX]], axis=-1)  75.1 us
    psum x1, waiting for transfers between devices, on_device(): atom_totals = lax.psum(partial_matrices, 'band')  66.1 us
    reduce_scatter x1, waiting for transfers between devices, on_device(): result = lax.psum_scatter(total, 'band', scatter_dimension=1, tiled=True)  43.9 us
    all_gather x1, blocking collectives, on_device(): every_box = lax.all_gather(box_part, 'grid', axis=0, tiled=True)  38.3 us
    dynamic_update_slice x7, local copies, waits for them, and re-layouts, place(): return lax.dynamic_update_slice(acc, current + pieces[index], corner)  30 us
  transfers between devices with their start and end apart: 4, of which 3 were waited for; matrix products, arithmetic and copies ran while one was open for 11% of the time, Pallas kernels for 0%

commit v1 on v0

v1 whole, which is shorter than its diff:
```python
import functools

import jax
import jax.numpy as jnp
import numpy as np
from jax import lax
from jax.experimental import pallas as pl
from jax.experimental.pallas import tpu as pltpu
from jax.sharding import PartitionSpec as P

GRID = 256
KG = 128
PLANES = 8
BOX = 16
NFUNC = 128
NBANDS = 8
N_GRID = 32
N_ATOMS = 64
OWN = 4
CAP = 688
NEAR = 6
BF = jnp.bfloat16
F32 = jnp.float32
VM = pl.BlockSpec(memory_space=pltpu.VMEM)
SM = pl.BlockSpec(memory_space=pltpu.SMEM)
ANY = pl.BlockSpec(memory_space=pl.ANY)
NT = (((1,), (1,)), ((), ()))
NN = (((1,), (0,)), ((), ()))


def tables():
    frequency = np.arange(KG) - KG // 2
    angles = 2.0 * np.pi * ((frequency[:, None] * np.arange(GRID)[None, :]) % GRID) / GRID
    cosine = np.cos(angles) * KG ** -0.5
    sine = np.sin(angles) * KG ** -0.5
    to_real = np.concatenate([cosine, -sine], axis=0)
    to_imag = np.concatenate([sine, cosine], axis=0)
    along_z = np.stack([to_real.T, to_imag.T]).reshape(2, N_GRID, PLANES, 2 * KG)
    along_z = along_z.transpose(1, 0, 2, 3).reshape(2 * GRID, 2 * KG)
    along_y = np.concatenate([to_real, to_imag], axis=1)
    along_x = np.concatenate([to_real.T, to_imag.T], axis=0)
    return along_z, along_y, along_x


def halves(table):
    high = table.astype(np.float32).astype(BF)
    low = (table - high.astype(np.float64)).astype(np.float32).astype(BF)
    return high, low


def split(value):
    high = value.astype(BF)
    return high, (value - high.astype(F32)).astype(BF)


def mm(left, right, dims=NN):
    return lax.dot_general(left, right, dims, preferred_element_type=F32)


def mm3(left, right, dims=NN):
    return mm(left[0], right[0], dims) + mm(left[1], right[0], dims) + mm(left[0], right[1], dims)


def z_kernel(c_ref, high_ref, low_ref, out_ref):
    both = jnp.concatenate([c_ref[0], c_ref[1]], axis=1)
    parts = split(both)
    for chunk in range(4):
        rows = pl.ds(chunk * 128, 128)
        got = mm3((high_ref[rows, :], low_ref[rows, :]), parts, NT)
        out_ref[pl.ds(chunk * 8, 8)] = got.reshape(8, 16, CAP)


def z_transform(coeffs, high, low):
    return pl.pallas_call(
        z_kernel,
        out_shape=jax.ShapeDtypeStruct((N_GRID, 16, CAP), F32),
        in_specs=[VM] * 3,
        out_specs=VM,
        name="z_transform",
    )(coeffs, high, low)


def exchange_kernel(in_ref, out_ref, own, local_sem, send_sem, recv_sem):
    me = lax.axis_index("grid")
    barrier = pltpu.get_barrier_semaphore()

    def peer(step):
        dz, dy = step // 4, step % 4
        return ((me // 4 + dz) % 8) * 4 + (me % 4 + dy) % 4

    for step in range(1, N_GRID):
        pl.semaphore_signal(barrier, inc=1, device_id={"grid": peer(step)})
    pl.semaphore_wait(barrier, N_GRID - 1)
    copies = []
    for step in ORDER:
        target = peer(step)
        copy = pltpu.make_async_remote_copy(
            src_ref=in_ref.at[target],
            dst_ref=out_ref.at[me],
            send_sem=send_sem.at[step],
            recv_sem=recv_sem.at[step],
            device_id={"grid": target},
        )
        copy.start()
        copies.append(copy)
    first = pltpu.make_async_copy(in_ref.at[me], own, local_sem)
    first.start()
    first.wait()
    second = pltpu.make_async_copy(own, out_ref.at[me], local_sem)
    second.start()
    second.wait()
    for copy in copies:
        copy.wait()


ORDER = sorted(range(1, N_GRID), key=lambda step: (-min(step // 4, 8 - step // 4), step % 4, step))


def exchange(sticks):
    return pl.pallas_call(
        exchange_kernel,
        out_shape=jax.ShapeDtypeStruct((N_GRID, 16, CAP), F32),
        in_specs=[ANY],
        out_specs=ANY,
        scratch_shapes=[
            pltpu.VMEM((16, CAP), F32),
            pltpu.SemaphoreType.DMA,
            pltpu.SemaphoreType.DMA((N_GRID,)),
            pltpu.SemaphoreType.DMA((N_GRID,)),
        ],
        compiler_params=pltpu.CompilerParams(collective_id=0, has_side_effects=True),
        name="stick_exchange",
    )(sticks)


def window_pick(y0):
    cell = lax.broadcasted_iota(jnp.int32, (GRID, GRID), 1)
    place = lax.broadcasted_iota(jnp.int32, (GRID, GRID), 0)
    return (place == (y0 + cell % BOX) % GRID).astype(F32).astype(BF)


def wave_kernel(ids, offsets, weight, sticks, yh, yl, xh, xl, aug, dens, proj, stage, cols, lhs_h, lhs_l, spec, wave, rows):
    me = lax.axis_index("grid")

    def one_source(source, carry):
        for first in range(0, CAP, 128):
            size = min(128, CAP - first)
            block = sticks[source, :, pl.ds(first, size)]
            wide = jnp.broadcast_to(block[:, None, :], (16, 8, size)).reshape(128, size)
            stage[pl.ds(first, size), :] = jnp.transpose(wide)
        base = source * CAP
        for first in range(0, CAP, 16):
            held = [stage[pl.ds(first + j, 1), :] for j in range(16)]
            for j in range(16):
                cols[pl.ds(ids[base + first + j] + 8, 1), :] = held[j]
        return carry

    lax.fori_loop(0, N_GRID, one_source, 0)

    lane = lax.broadcasted_iota(jnp.int32, (128, 128), 1) % 8

    def pack(block, carry):
        packed = cols[pl.ds(pl.multiple_of(block * 1024 + 8, 8), 128), :]
        for k in range(1, 8):
            here = cols[pl.ds(pl.multiple_of(block * 1024 + 8 + k * 128, 8), 128), :]
            packed = jnp.where(lane == k, here, packed)
        turned = jnp.transpose(packed)
        both = jnp.concatenate([turned[:64], turned[64:]], axis=1)
        high, low = split(both)
        where = pl.ds(pl.multiple_of(block * 64, 64), 64)
        lhs_h[where, :] = high
        lhs_l[where, :] = low
        return carry

    lax.fori_loop(0, 16, pack, 0)

    def y_step(chunk, carry):
        where = pl.ds(pl.multiple_of(chunk * 256, 256), 256)
        got = mm3((lhs_h[where, :], lhs_l[where, :]), (yh[...], yl[...]))
        got = got.reshape(4, 8, 8, 512)
        for part in range(4):
            first = pl.multiple_of(chunk * 32 + part * 8, 8)
            spec[:, pl.ds(first, 8), :] = got[part, :, :, :GRID]
            spec[:, pl.ds(first + KG, 8), :] = got[part, :, :, GRID:]
        return carry

    lax.fori_loop(0, 4, y_step, 0)

    scale = weight[0]

    def x_step(plane, carry):
        got = mm3((xh[...], xl[...]), split(spec[plane]))
        real, imag = got[:GRID], got[GRID:]
        wave[plane, 0, pl.ds(0, GRID), :] = real
        wave[plane, 1, pl.ds(0, GRID), :] = imag
        wave[plane, 0, pl.ds(GRID, 24), :] = real[:24]
        wave[plane, 1, pl.ds(GRID, 24), :] = imag[:24]
        dens[plane] = scale * (real * real + imag * imag)
        return carry

    lax.fori_loop(0, PLANES, x_step, 0)

    rows[...] = jnp.zeros_like(rows)
    cell = lax.broadcasted_iota(jnp.int32, (24, GRID), 1) // BOX
    row = lax.broadcasted_iota(jnp.int32, (24, GRID), 0)

    def one_atom(m, carry):
        atom = (2 * me - 4 + m + N_ATOMS) % N_ATOMS
        x0, y0, z0 = offsets[3 * atom], offsets[3 * atom + 1], offsets[3 * atom + 2]
        low_x = pl.multiple_of((x0 // 8) * 8, 8)
        window = wave[:, :, pl.ds(low_x, 24), :].reshape(16 * 24, GRID)
        high, low = split(window)
        pick = window_pick(y0)
        picked = (mm(high, pick) + mm(low, pick)).reshape(16, 24, GRID)
        keep = cell == row - (x0 - low_x)
        flat = jnp.sum(jnp.where(keep[None], picked, 0.0), axis=1)
        flat = flat.reshape(8, 2, GRID)
        for plane in range(PLANES):
            k = (me * PLANES + plane - z0 + GRID) % GRID

            @pl.when(k < BOX)
            def _():
                rows[k, pl.ds(2 * m, 2), :] = flat[plane]

        return carry

    for m in range(NEAR):
        one_atom(m, 0)

    def contract(k, total):
        return total + mm3(split(rows[k]), split(aug[k]), NT)

    proj[...] = lax.fori_loop(0, BOX, contract, jnp.zeros((16, NFUNC), F32))


def waves(ids, offsets, weight, sticks, yh, yl, xh, xl, aug):
    return pl.pallas_call(
        wave_kernel,
        out_shape=(
            jax.ShapeDtypeStruct((PLANES, GRID, GRID), F32),
            jax.ShapeDtypeStruct((16, NFUNC), F32),
        ),
        in_specs=[SM, SM, SM] + [VM] * 6,
        out_specs=(VM, VM),
        scratch_shapes=[
            pltpu.VMEM((CAP, 128), F32),
            pltpu.VMEM((KG * KG + 8, 128), F32),
            pltpu.VMEM((1024, GRID), BF),
            pltpu.VMEM((1024, GRID), BF),
            pltpu.VMEM((PLANES, GRID, GRID), F32),
            pltpu.VMEM((PLANES, 2, GRID + 24, GRID), F32),
            pltpu.VMEM((BOX, 16, GRID), F32),
        ],
        name="waves",
    )(ids, offsets, weight, sticks, yh, yl, xh, xl, aug)


def spread_kernel(proj, dens, every, slabs, own, local_sem, proj_send, proj_recv, dens_send, dens_recv):
    me = lax.axis_index("grid")
    band = lax.axis_index("band")
    barrier = pltpu.get_barrier_semaphore()
    for step in range(1, N_GRID):
        pl.semaphore_signal(barrier, inc=1, device_id={"grid": (me + step) % N_GRID})
    for step in range(1, NBANDS):
        pl.semaphore_signal(barrier, inc=1, device_id={"band": (band + step) % NBANDS})
    pl.semaphore_wait(barrier, N_GRID + NBANDS - 2)
    copies = []
    for step in range(1, N_GRID):
        target = (me + step) % N_GRID
        copies.append(
            pltpu.make_async_remote_copy(
                src_ref=proj,
                dst_ref=every.at[me],
                send_sem=proj_send.at[step],
                recv_sem=proj_recv.at[step],
                device_id={"grid": target},
            )
        )
    for step in range(1, NBANDS):
        target = (band + step) % NBANDS
        copies.append(
            pltpu.make_async_remote_copy(
                src_ref=dens.at[:, pl.ds(pl.multiple_of(target * 32, 32), 32), :],
                dst_ref=slabs.at[band],
                send_sem=dens_send.at[step],
                recv_sem=dens_recv.at[step],
                device_id={"band": target},
            )
        )
    for copy in copies:
        copy.start()
    every[me] = proj[...]
    first = pltpu.make_async_copy(dens.at[:, pl.ds(pl.multiple_of(band * 32, 32), 32), :], own, local_sem)
    first.start()
    first.wait()
    second = pltpu.make_async_copy(own, slabs.at[band], local_sem)
    second.start()
    second.wait()
    for copy in copies:
        copy.wait()


def spread(proj, dens):
    return pl.pallas_call(
        spread_kernel,
        out_shape=(
            jax.ShapeDtypeStruct((N_GRID, 16, NFUNC), F32),
            jax.ShapeDtypeStruct((NBANDS, PLANES, 32, GRID), F32),
        ),
        in_specs=[VM, ANY],
        out_specs=(VM, ANY),
        scratch_shapes=[
            pltpu.VMEM((PLANES, 32, GRID), F32),
            pltpu.SemaphoreType.DMA,
            pltpu.SemaphoreType.DMA((N_GRID,)),
            pltpu.SemaphoreType.DMA((N_GRID,)),
            pltpu.SemaphoreType.DMA((NBANDS,)),
            pltpu.SemaphoreType.DMA((NBANDS,)),
        ],
        compiler_params=pltpu.CompilerParams(collective_id=1, has_side_effects=True),
        name="spread",
    )(proj, dens)


def choose_kernel(slots, weight, every, out):
    me = lax.axis_index("grid")

    def gathered(atom):
        parity = atom % 2
        total = jnp.zeros((2, NFUNC), F32)
        for j in range(3):
            total = total + every[(atom // 2 + j) % N_GRID, pl.ds(2 * (4 - 2 * j) + 2 * parity, 2), :]
        return total

    for m in range(NEAR):
        out[pl.ds(2 * m, 2), :] = gathered((2 * me - 4 + m + N_ATOMS) % N_ATOMS)
    for s in range(OWN):
        atom = slots[me * OWN + s]
        found = gathered(jnp.maximum(atom, 0))
        out[pl.ds(12 + 2 * s, 2), :] = jnp.where(atom >= 0, found, 0.0)
    out[pl.ds(20, 4), :] = jnp.full((4, NFUNC), weight[0], F32)


def choose(slots, weight, every):
    return pl.pallas_call(
        choose_kernel,
        out_shape=jax.ShapeDtypeStruct((24, NFUNC), F32),
        in_specs=[SM, SM, VM],
        out_specs=VM,
        name="choose",
    )(slots, weight, every)


def share_kernel(mine, out, send_sem, recv_sem):
    band = lax.axis_index("band")
    barrier = pltpu.get_barrier_semaphore()
    for step in range(1, NBANDS):
        pl.semaphore_signal(barrier, inc=1, device_id={"band": (band + step) % NBANDS})
    pl.semaphore_wait(barrier, NBANDS - 1)
    copies = []
    for step in range(1, NBANDS):
        target = (band + step) % NBANDS
        copy = pltpu.make_async_remote_copy(
            src_ref=mine,
            dst_ref=out.at[band],
            send_sem=send_sem.at[step],
            recv_sem=recv_sem.at[step],
            device_id={"band": target},
        )
        copy.start()
        copies.append(copy)
    out[band] = mine[...]
    for copy in copies:
        copy.wait()


def share(mine):
    return pl.pallas_call(
        share_kernel,
        out_shape=jax.ShapeDtypeStruct((NBANDS, 24, NFUNC), F32),
        in_specs=[VM],
        out_specs=VM,
        scratch_shapes=[pltpu.SemaphoreType.DMA((NBANDS,)), pltpu.SemaphoreType.DMA((NBANDS,))],
        compiler_params=pltpu.CompilerParams(collective_id=2, has_side_effects=True),
        name="share",
    )(mine)


def final_kernel(offsets, shared, slabs, aug, dens, totals, near, level, boxes):
    me = lax.axis_index("grid")
    band = lax.axis_index("band")
    for m in range(NEAR):
        for b in range(NBANDS):
            near[pl.ds(m * 16 + 2 * b, 2), :] = shared[b, pl.ds(2 * m, 2), :]
    for b in range(NBANDS):
        level[pl.ds(2 * b, 2), :] = shared[b, pl.ds(20, 2), :]
    weights = level[...]
    for s in range(OWN):
        own = jnp.concatenate([shared[b, pl.ds(12 + 2 * s, 2), :] for b in range(NBANDS)], axis=0)
        totals[s] = lax.dot_general(
            own * weights,
            own,
            (((0,), (0,)), ((), ())),
            precision=lax.Precision.HIGHEST,
            preferred_element_type=F32,
        )
    parts = split(near[...])
    wide = jnp.concatenate([weights, weights], axis=1)

    def one_layer(k, carry):
        value = mm3(parts, split(aug[k])).reshape(NEAR, 16, GRID)
        boxes[k, pl.ds(0, NEAR), :] = jnp.sum(value * value * wide[None], axis=1)
        return carry

    lax.fori_loop(0, BOX, one_layer, 0)
    total = slabs[0]
    for b in range(1, NBANDS):
        total = total + slabs[b]
    dens[...] = total
    row = lax.broadcasted_iota(jnp.int32, (32, GRID), 0)
    cell = lax.broadcasted_iota(jnp.int32, (32, GRID), 1) // BOX
    for m in range(NEAR):
        atom = (2 * me - 4 + m + N_ATOMS) % N_ATOMS
        x0, y0, z0 = offsets[3 * atom], offsets[3 * atom + 1], offsets[3 * atom + 2]
        shift = (band * 32 - x0 + GRID) % GRID

        @pl.when((shift < BOX) | (shift > GRID - 32))
        def _():
            keep = cell == (row + shift) % GRID
            planes = []
            for plane in range(PLANES):
                k = (me * PLANES + plane - z0 + GRID) % GRID
                line = boxes[jnp.minimum(k, BOX - 1), pl.ds(m, 1), :]
                line = jnp.where(k < BOX, line, 0.0)
                planes.append(jnp.where(keep, line, 0.0))
            high, low = split(jnp.concatenate(planes, axis=0))
            pick = window_pick(y0)
            spot = mm(high, pick, NT) + mm(low, pick, NT)
            dens[...] += spot.reshape(PLANES, 32, GRID)


def final(offsets, shared, slabs, aug):
    return pl.pallas_call(
        final_kernel,
        out_shape=(
            jax.ShapeDtypeStruct((PLANES, 32, GRID), F32),
            jax.ShapeDtypeStruct((OWN, NFUNC, NFUNC), F32),
        ),
        in_specs=[SM, VM, VM, VM],
        out_specs=(VM, VM),
        scratch_shapes=[
            pltpu.VMEM((NEAR * 16, NFUNC), F32),
            pltpu.VMEM((16, NFUNC), F32),
            pltpu.VMEM((BOX, 8, GRID), F32),
        ],
        name="final",
    )(offsets, shared, slabs, aug)


def on_device(coeffs, stick_ids, band_weights, aug_functions, atom_offsets, intersection_list, atom_slots):
    along_z, along_y, along_x = (halves(table) for table in tables())
    offsets = atom_offsets.reshape(-1)
    aug = jnp.transpose(aug_functions, (1, 0, 2))
    sticks = z_transform(coeffs.reshape(2, CAP, KG), *along_z)
    received = exchange(sticks)
    dens, proj = waves(stick_ids, offsets, band_weights, received, *along_y, *along_x, aug)
    every, slabs = spread(proj, dens)
    shared = share(choose(atom_slots, band_weights, every))
    return final(offsets, shared, slabs, aug)


def solution(mesh):
    placed = (P(None, "band", "grid", None), P(), P("band"), P(), P(), P("grid", None), P())
    return jax.shard_map(
        on_device,
        mesh=mesh,
        in_specs=placed,
        out_specs=(P("grid", "band", None), P("grid", None, None)),
        check_vma=False,
    )
```

time: 800 us -> 148 us (0.18); the launches traced: 785 us -> 148 us
  local copies, waits for them, and re-layouts: 383 us -> 4 us
  waiting for transfers between devices: 248 us -> 0 us
  Pallas kernels: 0 us -> 143 us
  matrix products: 46 us -> 0 us
  blocking collectives: 38.3 us -> 0 us
  loops' own time: 26.6 us -> 0 us
  other arithmetic: 14.8 us -> 0 us
  between operations: 15.7 us -> 1.31 us
  starting transfers between devices: 12.4 us -> 0 us
    pallas_call x0 -> x7, Pallas kernels: none -> 143 us  [the longest x1 47.9 us: exchange(): pl.pallas_call(exchange_kernel, out_shape=jax.ShapeDtypeStruct((N_GRID, 1...]
    unnamed x4 -> x0, waiting for transfers between devices: 138 us -> none
    gather x3 -> x0, local copies, waits for them, and re-layouts: 125 us -> none  [the longest x1 119 us: on_device(): spectra = received[:, :, :, slot_map].reshape(2, bands_here, planes, KG, KG)]
    scatter x1 -> x0, local copies, waits for them, and re-layouts: 81.4 us -> none  [column_slots(): filled = jnp.zeros((total + 1,), jnp.int32).at[target].set(jnp.arange(sti...]
    concatenate x1 -> x0, local copies, waits for them, and re-layouts: 75.1 us -> none  [wrap_pad(): return jnp.concatenate([field, field[..., :BOX]], axis=-1)]
    psum x1 -> x0, waiting for transfers between devices: 66.1 us -> none  [on_device(): atom_totals = lax.psum(partial_matrices, 'band')]
    dot_general x19 -> x0, matrix products: 46 us -> none  [the longest x1 9.76 us: project_atom(): return jnp.einsum('ipc,xbpc->bxi', chosen, window, precision=HIGH)]
    reduce_scatter x1 -> x0, waiting for transfers between devices: 43.9 us -> none  [on_device(): result = lax.psum_scatter(total, 'band', scatter_dimension=1, tiled=True)]
  transfers between devices with their start and end apart: 4 -> 0, of which waited for: 3 -> 0; matrix products, arithmetic and copies ran while one was open for 11% -> 0% of each run, Pallas kernels for 0% -> 0%
where the time goes in v1:
time: 148 us
  Pallas kernels  143 us (97%)
  local copies, waits for them, and re-layouts  4 us (3%)
    pallas_call x1, Pallas kernels, exchange(): pl.pallas_call(exchange_kernel, out_shape=jax.ShapeDtypeStruct((N_GRID, 1...  47.9 us
    pallas_call x1, Pallas kernels, waves(): pl.pallas_call(wave_kernel, out_shape=(jax.ShapeDtypeStruct((PLANES, GRID...  42.6 us
    pallas_call x1, Pallas kernels, spread(): pl.pallas_call(spread_kernel, out_shape=(jax.ShapeDtypeStruct((N_GRID, 16...  32.8 us
    pallas_call x1, Pallas kernels, final(): pl.pallas_call(final_kernel, out_shape=(jax.ShapeDtypeStruct((PLANES, 32,...  7.16 us
    pallas_call x1, Pallas kernels, share(): pl.pallas_call(share_kernel, out_shape=jax.ShapeDtypeStruct((NBANDS, 24,...  6.67 us
    pallas_call x1, Pallas kernels, z_transform(): pl.pallas_call(z_kernel, out_shape=jax.ShapeDtypeStruct((N_GRID, 16, CAP)...  3.89 us
    unnamed x4, local copies, waits for them, and re-layouts  3.33 us

profile of v1, /device:TPU:1, one launch (start us, length us, event | category | flops | bytes accessed | tf_op | source)
XLA Modules:
  0.0 148.0 jit_solution(5731621849259093270)
XLA Ops:
  1.3 0.8 copy.15
  2.0 0.7 reshape.10.offsets
  2.7 3.9 %z_transform.1.in_ref = f32[32,16,688]{2,1,0:T(8,128)} custom-call(f32[2,688,128]{2,1,0:T(8,128)} %bitcast.6, bf16[512,256]{1,0:T(8,128)(2,1)} %constant.12.clone.high_ref, bf16[512,256]{1,0:T(8,128)(2,1)} %constant.13.clone.low_ref), custom_call_target="tpu_custom_call" | custom-call | tf_op jit(solution)/shard_map/z_transform/pallas_call | solution.py:74
  6.6 0.0 copy-start
  6.6 47.9 %stick_exchange.1.sticks = f32[32,16,688]{2,1,0:T(8,128)} custom-call(f32[32,16,688]{2,1,0:T(8,128)} %z_transform.1.in_ref), custom_call_target="tpu_custom_call" | custom-call | tf_op jit(solution)/shard_map/stick_exchange/pallas_call | solution.py:120
  54.5 0.0 copy-done
  54.5 2.6 %copy.18 = f32[128,16,256]{2,0,1:T(8,128)} copy(f32[128,16,256]{2,1,0:T(8,128)S(1)} %copy-done) | data formatting | bytes 4194304 | tf_op args[3]
  57.0 42.6 %waves.1 = (f32[8,256,256]{2,1,0:T(8,128)}, f32[16,128]{1,0:T(8,128)}) custom-call(s32[22016]{0:T(1024)} %ids.1, s32[192]{0:T(256)} %reshape.10.offsets, f32[1]{0:T(128)S(6)} %copy.19.weight, f32[32,16,688]{2,1,0:T(8,128)} %stick_exchange.1.sticks, bf16[256,512]{1,0:T(8,128)(2,1)} %constant.14.clone.yh, bf16[256,512]{1,0:T(8,128)(2,1)} %constant.15.clone.yl, ...), custom_call_target="tpu_custom_call" | custom-call | tf_op jit(solution)/shard_map/waves/pallas_call | solution.py:237
  99.7 32.8 %spread.1 = (f32[32,16,128]{2,1,0:T(8,128)}, f32[8,8,32,256]{3,2,1,0:T(8,128)}) custom-call(f32[16,128]{1,0:T(8,128)} %get-tuple-element.6.proj, f32[8,256,256]{2,1,0:T(8,128)} %get-tuple-element.7.dens), custom_call_target="tpu_custom_call" | custom-call | tf_op jit(solution)/shard_map/spread/pallas_call | solution.py:304
  132.4 1.7 %choose.1.mine = f32[24,128]{1,0:T(8,128)} custom-call(s32[128]{0:T(128)} %slots.1, f32[1]{0:T(128)S(6)} %copy.19.weight, f32[32,16,128]{2,1,0:T(8,128)} %get-tuple-element.8.every), custom_call_target="tpu_custom_call" | custom-call | tf_op jit(solution)/shard_map/choose/pallas_call | solution.py:345
  134.2 6.7 %share.1.shared = f32[8,24,128]{2,1,0:T(8,128)} custom-call(f32[24,128]{1,0:T(8,128)} %choose.1.mine), custom_call_target="tpu_custom_call" | custom-call | tf_op jit(solution)/shard_map/share/pallas_call | solution.py:378
  140.9 7.2 %final.1 = (f32[8,32,256]{2,1,0:T(8,128)}, f32[4,128,128]{2,1,0:T(8,128)}) custom-call(s32[192]{0:T(256)} %reshape.10.offsets, f32[8,24,128]{2,1,0:T(8,128)} %share.1.shared, f32[8,8,32,256]{3,2,1,0:T(8,128)} %get-tuple-element.9.slabs, f32[16,128,256]{2,1,0:T(8,128)} %bitcast.5), custom_call_target="tpu_custom_call" | custom-call | tf_op jit(solution)/shard_map/final/pallas_call | solution.py:443
Async XLA Ops:
  6.6 47.9 %copy-start = (f32[128,16,256]{2,1,0:T(8,128)S(1)}, f32[128,16,256]{2,1,0:T(8,128)}, u32[]{:S(2)}) copy-start(f32[128,16,256]{2,1,0:T(8,128)} %param.16) | copy-start | bytes 6291460

commit v2 on v1

v2 whole, which is shorter than its diff:
```python
import functools

import jax
import jax.numpy as jnp
import numpy as np
from jax import lax
from jax.experimental import pallas as pl
from jax.experimental.pallas import tpu as pltpu
from jax.sharding import PartitionSpec as P

GRID = 256
KG = 128
PLANES = 8
BOX = 16
NFUNC = 128
NBANDS = 8
N_GRID = 32
N_ATOMS = 64
OWN = 4
CAP = 688
NEAR = 6
HIGH = 64
FULL = CAP // 128
REST = CAP % 128
TILES = 2 * FULL + 1
BF = jnp.bfloat16
F32 = jnp.float32
VM = pl.BlockSpec(memory_space=pltpu.VMEM)
SM = pl.BlockSpec(memory_space=pltpu.SMEM)
ANY = pl.BlockSpec(memory_space=pl.ANY)
NT = (((1,), (1,)), ((), ()))
NN = (((1,), (0,)), ((), ()))


def tables():
    frequency = np.arange(KG) - KG // 2
    angles = 2.0 * np.pi * ((frequency[:, None] * np.arange(GRID)[None, :]) % GRID) / GRID
    cosine = np.cos(angles) * KG ** -0.5
    sine = np.sin(angles) * KG ** -0.5
    to_real = np.concatenate([cosine, -sine], axis=0)
    to_imag = np.concatenate([sine, cosine], axis=0)
    along_z = np.stack([to_real.T, to_imag.T]).reshape(2, N_GRID, PLANES, 2 * KG)
    along_z = along_z.transpose(1, 0, 2, 3).reshape(2 * GRID, 2 * KG)
    along_y = np.concatenate([to_real, to_imag], axis=1)
    order = np.concatenate([np.arange(0, KG, 2), np.arange(1, KG, 2)])
    order = np.concatenate([order, order + KG])
    along_x = np.concatenate([to_real.T, to_imag.T], axis=0)[:, order]
    return along_z, along_y, along_x


def halves(table):
    high = table.astype(np.float32).astype(BF)
    low = (table - high.astype(np.float64)).astype(np.float32).astype(BF)
    return high, low


def split(value):
    high = value.astype(BF)
    return high, (value - high.astype(F32)).astype(BF)


def mm(left, right, dims=NN):
    return lax.dot_general(left, right, dims, preferred_element_type=F32)


def mm3(left, right, dims=NN):
    return mm(left[0], right[0], dims) + mm(left[1], right[0], dims) + mm(left[0], right[1], dims)


def z_kernel(c_ref, high_ref, low_ref, out_ref):
    both = jnp.concatenate([c_ref[0], c_ref[1]], axis=1)
    parts = split(both)
    for chunk in range(4):
        rows = pl.ds(chunk * 128, 128)
        got = mm3((high_ref[rows, :], low_ref[rows, :]), parts, NT).reshape(8, 16, CAP)
        where = pl.ds(chunk * 8, 8)
        for tile in range(FULL):
            lanes = slice(tile * 128, tile * 128 + 128)
            out_ref[where, 2 * tile] = got[:, :8, lanes]
            out_ref[where, 2 * tile + 1] = got[:, 8:, lanes]
        rest = got[:, :, FULL * 128 :]
        blank = jnp.zeros((8, 8, 128 - 2 * REST), F32)
        out_ref[where, 2 * FULL] = jnp.concatenate([rest[:, :8], rest[:, 8:], blank], axis=2)


def z_transform(coeffs, high, low):
    return pl.pallas_call(
        z_kernel,
        out_shape=jax.ShapeDtypeStruct((N_GRID, TILES, 8, 128), F32),
        in_specs=[VM] * 3,
        out_specs=VM,
        name="z_transform",
    )(coeffs, high, low)


def exchange_kernel(ids, in_ref, aug, grid, aug_h, aug_l, land, held, local_sem, aug_sem, send_sem, recv_sem):
    me = lax.axis_index("grid")
    z, y = me // 4, me % 4
    barrier = pltpu.get_barrier_semaphore()

    def offset(step):
        turn = (step + 28) % N_GRID
        part = turn // 4
        return 4 + ((part + 1) // 2) * (1 - 2 * (part % 2)), turn % 4

    def copy_at(step):
        dz, dy = offset(step)
        target = ((z + dz) % 8) * 4 + (y + dy) % 4
        return pltpu.make_async_remote_copy(
            src_ref=in_ref.at[target],
            dst_ref=land.at[me],
            send_sem=send_sem.at[step],
            recv_sem=recv_sem.at[step],
            device_id={"grid": target},
        )

    for step in range(1, N_GRID):
        pl.semaphore_signal(barrier, inc=1, device_id={"grid": (me + step) % N_GRID})
    pl.semaphore_wait(barrier, N_GRID - 1)
    for step in range(1, N_GRID):
        copy_at(step).start()
    mine = pltpu.make_async_copy(in_ref.at[me], land.at[me], local_sem)
    mine.start()
    fetch = pltpu.make_async_copy(aug, held, aug_sem)
    fetch.start()
    grid[...] = jnp.zeros_like(grid)
    mine.wait()
    fetch.wait()
    for k in range(BOX):
        high, low = split(held[:, k, :])
        aug_h[k] = high
        aug_l[k] = low

    row = lax.broadcasted_iota(jnp.int32, (HIGH, CAP), 0)
    column = lax.broadcasted_iota(jnp.int32, (GRID, CAP), 0)

    def one_source(step, carry):
        @pl.when(step > 0)
        def _():
            copy_at(step).wait()

        dz, dy = offset(step)
        source = ((z - dz + 8) % 8) * 4 + (y - dy + 4) % 4
        name = ids[source]
        in_row = (row == (name >> 8)).astype(F32).astype(BF)
        in_column = (column == (name & (GRID - 1))).astype(F32).astype(BF)
        tiles = land[source]
        top = [tiles[2 * tile] for tile in range(FULL)] + [tiles[2 * FULL][:, :REST]]
        bottom = [tiles[2 * tile + 1] for tile in range(FULL)] + [tiles[2 * FULL][:, REST : 2 * REST]]
        value = jnp.concatenate([jnp.concatenate(top, axis=1), jnp.concatenate(bottom, axis=1)], axis=0)
        both = jnp.concatenate(split(value), axis=0)
        left = (in_row[None] * both[:, None, :]).reshape(32 * HIGH, CAP)
        got = mm(left, in_column, NT)
        grid[...] += (got[: 16 * HIGH] + got[16 * HIGH :]).reshape(16, HIGH, GRID)
        return carry

    lax.fori_loop(0, N_GRID, one_source, 0)


def exchange(ids, sticks, aug):
    return pl.pallas_call(
        exchange_kernel,
        out_shape=(
            jax.ShapeDtypeStruct((16, HIGH, GRID), F32),
            jax.ShapeDtypeStruct((BOX, NFUNC, GRID), BF),
            jax.ShapeDtypeStruct((BOX, NFUNC, GRID), BF),
        ),
        in_specs=[VM, ANY, ANY],
        out_specs=(VM, VM, VM),
        scratch_shapes=[
            pltpu.VMEM((N_GRID, TILES, 8, 128), F32),
            pltpu.VMEM((NFUNC, BOX, GRID), F32),
            pltpu.SemaphoreType.DMA,
            pltpu.SemaphoreType.DMA,
            pltpu.SemaphoreType.DMA((N_GRID,)),
            pltpu.SemaphoreType.DMA((N_GRID,)),
        ],
        compiler_params=pltpu.CompilerParams(collective_id=0, has_side_effects=True),
        name="stick_exchange",
    )(ids, sticks, aug)


def window_pick(y0):
    cell = lax.broadcasted_iota(jnp.int32, (GRID, GRID), 1)
    place = lax.broadcasted_iota(jnp.int32, (GRID, GRID), 0)
    return (place == (y0 + cell % BOX) % GRID).astype(F32).astype(BF)


def wave_kernel(offsets, weight, grid, yh, yl, xh, xl, aug_h, aug_l, dens, proj, spec, wave, rows):
    me = lax.axis_index("grid")
    for parity in range(2):
        lanes = slice(parity * KG, parity * KG + KG)
        both = jnp.concatenate([grid[:8, :, lanes], grid[8:, :, lanes]], axis=2).reshape(8 * HIGH, GRID)
        got = mm3(split(both), (yh[...], yl[...])).reshape(8, HIGH, 2 * GRID)
        spec[:, pl.ds(parity * HIGH, HIGH), :] = got[:, :, :GRID]
        spec[:, pl.ds(parity * HIGH + KG, HIGH), :] = got[:, :, GRID:]

    scale = weight[0]

    def x_step(plane, carry):
        got = mm3((xh[...], xl[...]), split(spec[plane]))
        real, imag = got[:GRID], got[GRID:]
        wave[plane, 0, pl.ds(0, GRID), :] = real
        wave[plane, 1, pl.ds(0, GRID), :] = imag
        wave[plane, 0, pl.ds(GRID, 24), :] = real[:24]
        wave[plane, 1, pl.ds(GRID, 24), :] = imag[:24]
        local = (scale * (real * real + imag * imag)).reshape(4, 2, 32, GRID)
        dens[0, :, plane] = local[:, 0]
        dens[1, :, plane] = local[:, 1]
        return carry

    lax.fori_loop(0, PLANES, x_step, 0)

    rows[...] = jnp.zeros_like(rows)
    cell = lax.broadcasted_iota(jnp.int32, (24, GRID), 1) // BOX
    row = lax.broadcasted_iota(jnp.int32, (24, GRID), 0)

    def one_atom(m, carry):
        atom = (2 * me - 4 + m + N_ATOMS) % N_ATOMS
        x0, y0, z0 = offsets[0, atom], offsets[1, atom], offsets[2, atom]
        low_x = pl.multiple_of((x0 // 8) * 8, 8)
        window = wave[:, :, pl.ds(low_x, 24), :].reshape(16 * 24, GRID)
        high, low = split(window)
        pick = window_pick(y0)
        picked = (mm(high, pick) + mm(low, pick)).reshape(16, 24, GRID)
        keep = cell == row - (x0 - low_x)
        flat = jnp.sum(jnp.where(keep[None], picked, 0.0), axis=1)
        flat = flat.reshape(8, 2, GRID)
        for plane in range(PLANES):
            k = (me * PLANES + plane - z0 + GRID) % GRID

            @pl.when(k < BOX)
            def _():
                rows[k, pl.ds(2 * m, 2), :] = flat[plane]

        return carry

    for m in range(NEAR):
        one_atom(m, 0)

    def contract(k, total):
        return total + mm3(split(rows[k]), (aug_h[k], aug_l[k]), NT)

    proj[...] = lax.fori_loop(0, BOX, contract, jnp.zeros((16, NFUNC), F32))


def waves(offsets, weight, grid, yh, yl, xh, xl, aug_h, aug_l):
    return pl.pallas_call(
        wave_kernel,
        out_shape=(
            jax.ShapeDtypeStruct((2, 4, PLANES, 32, GRID), F32),
            jax.ShapeDtypeStruct((16, NFUNC), F32),
        ),
        in_specs=[SM, SM] + [VM] * 7,
        out_specs=(VM, VM),
        scratch_shapes=[
            pltpu.VMEM((PLANES, GRID, GRID), F32),
            pltpu.VMEM((PLANES, 2, GRID + 24, GRID), F32),
            pltpu.VMEM((BOX, 16, GRID), F32),
        ],
        name="waves",
    )(offsets, weight, grid, yh, yl, xh, xl, aug_h, aug_l)


def sum_kernel(
    slots, weight, proj, dens, aug_h, aug_l, total, shared, boxes,
    every, mine, near, level, half, other, summed, slabs,
    half_sem, pair_send, pair_recv, slab_send, slab_recv, proj_send, proj_recv, share_send, share_recv,
):
    me = lax.axis_index("grid")
    band = lax.axis_index("band")
    chip, core = band // 2, band % 2
    partner = chip * 2 + 1 - core
    barrier = pltpu.get_barrier_semaphore()
    for step in range(1, N_GRID):
        pl.semaphore_signal(barrier, inc=1, device_id={"grid": (me + step) % N_GRID})
    for step in range(1, NBANDS):
        pl.semaphore_signal(barrier, inc=1, device_id={"band": (band + step) % NBANDS})
    fetches = []
    for step in range(4):
        place = (chip + step) % 4
        fetches.append(pltpu.make_async_copy(dens.at[core, place], half.at[step], half_sem.at[step]))
        fetches[-1].start()
    pl.semaphore_wait(barrier, N_GRID + NBANDS - 2)

    pairs, slab_copies = [], []
    for step in range(4):
        place = (chip + step) % 4
        pairs.append(
            pltpu.make_async_remote_copy(
                src_ref=dens.at[1 - core, place],
                dst_ref=other.at[step],
                send_sem=pair_send.at[step],
                recv_sem=pair_recv.at[step],
                device_id={"band": partner},
            )
        )
        slab_copies.append(
            None
            if step == 0
            else pltpu.make_async_remote_copy(
                src_ref=summed.at[step],
                dst_ref=slabs.at[step],
                send_sem=slab_send.at[step],
                recv_sem=slab_recv.at[step],
                device_id={"band": place * 2 + core},
            )
        )
    pairs[2].start()
    proj_copies = []
    for step in range(1, N_GRID):
        copy = pltpu.make_async_remote_copy(
            src_ref=proj,
            dst_ref=every.at[me],
            send_sem=proj_send.at[step],
            recv_sem=proj_recv.at[step],
            device_id={"grid": (me + step) % N_GRID},
        )
        copy.start()
        proj_copies.append(copy)
    for step in (1, 3, 0):
        pairs[step].start()
    every[me] = proj[...]

    def combine(step):
        fetches[step].wait()
        pairs[step].wait()
        summed[step] = half[step] + other[step]

    combine(2)
    slab_copies[2].start()
    for copy in proj_copies:
        copy.wait()

    def gathered(atom):
        parity = atom % 2
        found = jnp.zeros((2, NFUNC), F32)
        for j in range(3):
            found = found + every[(atom // 2 + j) % N_GRID, pl.ds(2 * (4 - 2 * j) + 2 * parity, 2), :]
        return found

    for m in range(NEAR):
        mine[pl.ds(2 * m, 2), :] = gathered((2 * me - 4 + m + N_ATOMS) % N_ATOMS)
    for s in range(OWN):
        atom = slots[me * OWN + s]
        found = gathered(jnp.maximum(atom, 0))
        mine[pl.ds(12 + 2 * s, 2), :] = jnp.where(atom >= 0, found, 0.0)
    mine[pl.ds(20, 4), :] = jnp.full((4, NFUNC), weight[0], F32)
    share_copies = []
    for step in range(1, NBANDS):
        copy = pltpu.make_async_remote_copy(
            src_ref=mine,
            dst_ref=shared.at[band],
            send_sem=share_send.at[step],
            recv_sem=share_recv.at[step],
            device_id={"band": (band + step) % NBANDS},
        )
        copy.start()
        share_copies.append(copy)
    for step in (1, 3):
        combine(step)
        slab_copies[step].start()
    combine(0)
    shared[band] = mine[...]
    for copy in share_copies:
        copy.wait()
    for b in range(NBANDS):
        for m in range(NEAR):
            near[pl.ds(m * 16 + 2 * b, 2), :] = shared[b, pl.ds(2 * m, 2), :]
        level[pl.ds(2 * b, 2), :] = shared[b, pl.ds(20, 2), :]
    weights = level[...]
    parts = split(near[...])
    wide = jnp.concatenate([weights, weights], axis=1)

    def one_layer(k, carry):
        value = mm3(parts, (aug_h[k], aug_l[k])).reshape(NEAR, 16, GRID)
        boxes[k, pl.ds(0, NEAR), :] = jnp.sum(value * value * wide[None], axis=1)
        return carry

    lax.fori_loop(0, BOX, one_layer, 0)
    for step in (1, 2, 3):
        slab_copies[step].wait()
    total[...] = (summed[0] + slabs[1]) + (slabs[2] + slabs[3])


def sums(slots, weight, proj, dens, aug_h, aug_l):
    quarter = (PLANES, 32, GRID)
    dma = pltpu.SemaphoreType.DMA
    return pl.pallas_call(
        sum_kernel,
        out_shape=(
            jax.ShapeDtypeStruct(quarter, F32),
            jax.ShapeDtypeStruct((NBANDS, 24, NFUNC), F32),
            jax.ShapeDtypeStruct((BOX, 8, GRID), F32),
        ),
        in_specs=[SM, SM, VM, ANY, VM, VM],
        out_specs=(VM, VM, VM),
        scratch_shapes=[
            pltpu.VMEM((N_GRID, 16, NFUNC), F32),
            pltpu.VMEM((24, NFUNC), F32),
            pltpu.VMEM((NEAR * 16, NFUNC), F32),
            pltpu.VMEM((16, NFUNC), F32),
            pltpu.VMEM((4,) + quarter, F32),
            pltpu.VMEM((4,) + quarter, F32),
            pltpu.VMEM((4,) + quarter, F32),
            pltpu.VMEM((4,) + quarter, F32),
            dma((4,)), dma((4,)), dma((4,)), dma((4,)), dma((4,)),
            dma((N_GRID,)), dma((N_GRID,)), dma((NBANDS,)), dma((NBANDS,)),
        ],
        compiler_params=pltpu.CompilerParams(collective_id=1, has_side_effects=True),
        name="sums",
    )(slots, weight, proj, dens, aug_h, aug_l)


def final_kernel(offsets, shared, total, boxes, dens, totals):
    me = lax.axis_index("grid")
    band = lax.axis_index("band")
    weights = jnp.concatenate([shared[b, pl.ds(20, 2), :] for b in range(NBANDS)], axis=0)
    for s in range(OWN):
        own = jnp.concatenate([shared[b, pl.ds(12 + 2 * s, 2), :] for b in range(NBANDS)], axis=0)
        totals[s] = lax.dot_general(
            own * weights,
            own,
            (((0,), (0,)), ((), ())),
            precision=lax.Precision.HIGHEST,
            preferred_element_type=F32,
        )
    dens[...] = total[...]
    row = lax.broadcasted_iota(jnp.int32, (32, GRID), 0)
    cell = lax.broadcasted_iota(jnp.int32, (32, GRID), 1) // BOX
    for m in range(NEAR):
        atom = (2 * me - 4 + m + N_ATOMS) % N_ATOMS
        x0, y0, z0 = offsets[0, atom], offsets[1, atom], offsets[2, atom]
        shift = (band * 32 - x0 + GRID) % GRID

        @pl.when((shift < BOX) | (shift > GRID - 32))
        def _():
            keep = cell == (row + shift) % GRID
            planes = []
            for plane in range(PLANES):
                k = (me * PLANES + plane - z0 + GRID) % GRID
                line = boxes[jnp.minimum(k, BOX - 1), pl.ds(m, 1), :]
                line = jnp.where(k < BOX, line, 0.0)
                planes.append(jnp.where(keep, line, 0.0))
            high, low = split(jnp.concatenate(planes, axis=0))
            pick = window_pick(y0)
            spot = mm(high, pick, NT) + mm(low, pick, NT)
            dens[...] += spot.reshape(PLANES, 32, GRID)


def final(offsets, shared, total, boxes):
    return pl.pallas_call(
        final_kernel,
        out_shape=(
            jax.ShapeDtypeStruct((PLANES, 32, GRID), F32),
            jax.ShapeDtypeStruct((OWN, NFUNC, NFUNC), F32),
        ),
        in_specs=[SM, VM, VM, VM],
        out_specs=(VM, VM),
        name="final",
    )(offsets, shared, total, boxes)


def on_device(coeffs, stick_ids, band_weights, aug_functions, atom_offsets, intersection_list, atom_slots):
    along_z, along_y, along_x = (halves(table) for table in tables())
    offsets = atom_offsets.T
    sticks = z_transform(coeffs.reshape(2, CAP, KG), *along_z)
    grid, aug_h, aug_l = exchange(stick_ids.reshape(N_GRID, 1, CAP), sticks, aug_functions)
    dens, proj = waves(offsets, band_weights, grid, *along_y, *along_x, aug_h, aug_l)
    total, shared, boxes = sums(atom_slots, band_weights, proj, dens, aug_h, aug_l)
    return final(offsets, shared, total, boxes)


def solution(mesh):
    placed = (P(None, "band", "grid", None), P(), P("band"), P(), P(), P("grid", None), P())
    return jax.shard_map(
        on_device,
        mesh=mesh,
        in_specs=placed,
        out_specs=(P("grid", "band", None), P("grid", None, None)),
        check_vma=False,
    )
```

time: 148 us -> 107 us (0.72)
  Pallas kernels: 143 us -> 104 us
  local copies, waits for them, and re-layouts: 4 us -> 1.71 us
    pallas_call x6 -> x4, Pallas kernels: 136 us -> 102 us  [the longest x1 54.6 us: exchange(): pl.pallas_call(exchange_kernel, out_shape=(jax.ShapeDtypeStruct((16, HIGH...]
    pallas_call x1, Pallas kernels: 7.16 us -> 2.34 us  [final(): pl.pallas_call(final_kernel, out_shape=(jax.ShapeDtypeStruct((PLANES, 32,...]
    unnamed x4 -> x0, local copies, waits for them, and re-layouts: 3.33 us -> none
where the time goes in v2:
time: 107 us
  Pallas kernels  104 us (97%)
  local copies, waits for them, and re-layouts  1.71 us (2%)
  between operations  1.29 us (1%)
    pallas_call x1, Pallas kernels, exchange(): pl.pallas_call(exchange_kernel, out_shape=(jax.ShapeDtypeStruct((16, HIGH...  54.6 us
    pallas_call x1, Pallas kernels, sums(): pl.pallas_call(sum_kernel, out_shape=(jax.ShapeDtypeStruct(quarter, F32),...  29.8 us
    pallas_call x1, Pallas kernels, waves(): pl.pallas_call(wave_kernel, out_shape=(jax.ShapeDtypeStruct((2, 4, PLANES...  13.1 us
    pallas_call x1, Pallas kernels, z_transform(): pl.pallas_call(z_kernel, out_shape=jax.ShapeDtypeStruct((N_GRID, TILES, 8...  3.94 us
    pallas_call x1, Pallas kernels, final(): pl.pallas_call(final_kernel, out_shape=(jax.ShapeDtypeStruct((PLANES, 32,...  2.34 us

profile of v2, /device:TPU:1, one launch (start us, length us, event | category | flops | bytes accessed | tf_op | source)
XLA Modules:
  0.0 106.9 jit_solution(4027276559720736377)
XLA Ops:
  1.3 1.7 %reshape.10.ids = s32[32,1,688]{2,1,0:T(1,128)} reshape(s32[22016]{0:T(1024)} %param.14) | data formatting | bytes 176128 | tf_op jit(solution)/shard_map/reshape | solution.py:468
  3.0 3.9 %z_transform.1.in_ref = f32[32,11,8,128]{3,2,1,0:T(8,128)} custom-call(f32[2,688,128]{2,1,0:T(8,128)} %bitcast.2, bf16[512,256]{1,0:T(8,128)(2,1)} %constant.12.clone.high_ref, bf16[512,256]{1,0:T(8,128)(2,1)} %constant.13.clone.low_ref), custom_call_target="tpu_custom_call" | custom-call | tf_op jit(solution)/shard_map/z_transform/pallas_call | solution.py:87
  6.9 54.6 %stick_exchange.1 = (f32[16,64,256]{2,1,0:T(8,128)}, bf16[16,128,256]{2,1,0:T(8,128)(2,1)}, bf16[16,128,256]{2,1,0:T(8,128)(2,1)}) custom-call(s32[32,1,688]{2,1,0:T(1,128)} %reshape.10.ids, f32[32,11,8,128]{3,2,1,0:T(8,128)} %z_transform.1.in_ref, f32[128,16,256]{2,1,0:T(8,128)} %aug.1), custom_call_target="tpu_custom_call" | custom-call | tf_op jit(solution)/shard_map/stick_exchange/pallas_call | solution.py:161
  61.6 13.1 %waves.1 = (f32[2,4,8,32,256]{4,3,2,1,0:T(8,128)}, f32[16,128]{1,0:T(8,128)}) custom-call(s32[3,64]{1,0:T(4,128)} %bitcast.3, f32[1]{0:T(128)S(6)} %copy.14.weight, f32[16,64,256]{2,1,0:T(8,128)} %get-tuple-element.10.grid, bf16[256,512]{1,0:T(8,128)(2,1)} %constant.14.clone.yh, bf16[256,512]{1,0:T(8,128)(2,1)} %constant.15.clone.yl, ...), custom_call_target="tpu_custom_call" | custom-call | tf_op jit(solution)/shard_map/waves/pallas_call | solution.py:248
  74.7 29.8 %sums.1 = (f32[8,32,256]{2,1,0:T(8,128)}, f32[8,24,128]{2,1,0:T(8,128)}, f32[16,8,256]{2,1,0:T(8,128)}) custom-call(s32[128]{0:T(128)} %slots.1, f32[1]{0:T(128)S(6)} %copy.14.weight, f32[16,128]{1,0:T(8,128)} %get-tuple-element.13.proj, f32[2,4,8,32,256]{4,3,2,1,0:T(8,128)} %get-tuple-element.14.dens, bf16[16,128,256]{2,1,0:T(8,128)(2,1)} %get-tuple-element.11.aug_h, ...), custom_call_target="tpu_custom_call" | custom-call | tf_op jit(solution)/shard_map/sums/pallas_call | solution.py:389
  104.5 2.3 %final.1 = (f32[8,32,256]{2,1,0:T(8,128)}, f32[4,128,128]{2,1,0:T(8,128)}) custom-call(s32[3,64]{1,0:T(4,128)} %bitcast.4, f32[8,24,128]{2,1,0:T(8,128)} %get-tuple-element.15.shared, f32[8,32,256]{2,1,0:T(8,128)} %get-tuple-element.16.total, f32[16,8,256]{2,1,0:T(8,128)} %get-tuple-element.17.boxes), custom_call_target="tpu_custom_call" | custom-call | tf_op jit(solution)/shard_map/final/pallas_call | solution.py:452

commit v3 on v2

--- a/solution.py
+++ b/solution.py
@@ -23,6 +23,7 @@
 FULL = CAP // 128
 REST = CAP % 128
 TILES = 2 * FULL + 1
+WIDE = FULL * 128 + 128
 BF = jnp.bfloat16
 F32 = jnp.float32
 VM = pl.BlockSpec(memory_space=pltpu.VMEM)
@@ -67,97 +68,111 @@
     return mm(left[0], right[0], dims) + mm(left[1], right[0], dims) + mm(left[0], right[1], dims)
 
 
-def z_kernel(c_ref, high_ref, low_ref, out_ref):
-    both = jnp.concatenate([c_ref[0], c_ref[1]], axis=1)
-    parts = split(both)
-    for chunk in range(4):
-        rows = pl.ds(chunk * 128, 128)
-        got = mm3((high_ref[rows, :], low_ref[rows, :]), parts, NT).reshape(8, 16, CAP)
+def exchange_kernel(
+    coeffs, table_h, table_l, ids, aug, grid, aug_h, aug_l,
+    sticks, land, names, held, part_h, part_l, aug_sem, send_sem, recv_sem,
+):
+    me = lax.axis_index("grid")
+    z, y = me // 4, me % 4
+    barrier = pltpu.get_barrier_semaphore()
+
+    def offset(step):
+        ring, turn = (step + 4) // 8, (step + 4) % 8
+        edge = 1 - ((ring % 4) + 3) // 4
+        dz = (ring * (1 - 2 * ((1 - edge) * (turn % 2))) + 8) % 8
+        return dz, edge * (turn % 4) + (1 - edge) * (turn // 2)
+
+    def target_at(step):
+        dz, dy = offset(step)
+        return ((z + dz) % 8) * 4 + (y + dy) % 4
+
+    def copy_at(step):
+        return pltpu.make_async_remote_copy(
+            src_ref=sticks.at[step],
+            dst_ref=land.at[step],
+            send_sem=send_sem.at[step],
+            recv_sem=recv_sem.at[step],
+            device_id={"grid": target_at(step)},
+        )
+
+    for step in range(1, N_GRID):
+        pl.semaphore_signal(barrier, inc=1, device_id={"grid": target_at(step)})
+    fetch = pltpu.make_async_copy(aug, held, aug_sem)
+    fetch.start()
+    high, low = split(jnp.concatenate([coeffs[0], coeffs[1]], axis=1))
+    part_h[...] = high
+    part_l[...] = low
+
+    def z_chunk(chunk):
+        rows = [pl.ds(pl.multiple_of(target_at(chunk * 8 + j) * 16, 16), 16) for j in range(8)]
+        left = (
+            jnp.concatenate([table_h[r, :] for r in rows], axis=0),
+            jnp.concatenate([table_l[r, :] for r in rows], axis=0),
+        )
+        got = mm3(left, (part_h[...], part_l[...]), NT).reshape(8, 16, CAP)
         where = pl.ds(chunk * 8, 8)
         for tile in range(FULL):
             lanes = slice(tile * 128, tile * 128 + 128)
-            out_ref[where, 2 * tile] = got[:, :8, lanes]
-            out_ref[where, 2 * tile + 1] = got[:, 8:, lanes]
+            sticks[where, 2 * tile] = got[:, :8, lanes]
+            sticks[where, 2 * tile + 1] = got[:, 8:, lanes]
         rest = got[:, :, FULL * 128 :]
         blank = jnp.zeros((8, 8, 128 - 2 * REST), F32)
-        out_ref[where, 2 * FULL] = jnp.concatenate([rest[:, :8], rest[:, 8:], blank], axis=2)
-
-
-def z_transform(coeffs, high, low):
-    return pl.pallas_call(
-        z_kernel,
-        out_shape=jax.ShapeDtypeStruct((N_GRID, TILES, 8, 128), F32),
-        in_specs=[VM] * 3,
-        out_specs=VM,
-        name="z_transform",
-    )(coeffs, high, low)
-
-
-def exchange_kernel(ids, in_ref, aug, grid, aug_h, aug_l, land, held, local_sem, aug_sem, send_sem, recv_sem):
-    me = lax.axis_index("grid")
-    z, y = me // 4, me % 4
-    barrier = pltpu.get_barrier_semaphore()
-
-    def offset(step):
-        turn = (step + 28) % N_GRID
-        part = turn // 4
-        return 4 + ((part + 1) // 2) * (1 - 2 * (part % 2)), turn % 4
-
-    def copy_at(step):
-        dz, dy = offset(step)
-        target = ((z + dz) % 8) * 4 + (y + dy) % 4
-        return pltpu.make_async_remote_copy(
-            src_ref=in_ref.at[target],
-            dst_ref=land.at[me],
-            send_sem=send_sem.at[step],
-            recv_sem=recv_sem.at[step],
-            device_id={"grid": target},
-        )
-
-    for step in range(1, N_GRID):
-        pl.semaphore_signal(barrier, inc=1, device_id={"grid": (me + step) % N_GRID})
+        sticks[where, 2 * FULL] = jnp.concatenate([rest[:, :8], rest[:, 8:], blank], axis=2)
+
+    z_chunk(0)
+    z_chunk(1)
     pl.semaphore_wait(barrier, N_GRID - 1)
-    for step in range(1, N_GRID):
-        copy_at(step).start()
-    mine = pltpu.make_async_copy(in_ref.at[me], land.at[me], local_sem)
-    mine.start()
-    fetch = pltpu.make_async_copy(aug, held, aug_sem)
-    fetch.start()
+    for chunk in range(4):
+        for step in range(max(1, chunk * 8), chunk * 8 + 8):
+            copy_at(step).start()
+        if chunk < 2:
+            z_chunk(chunk + 2)
+        elif chunk == 2:
+            land[0] = sticks[0]
+            names[...] = jnp.full_like(names, -1)
+            for source in range(N_GRID):
+                first, shift = source * CAP // 128, source * CAP % 128
+                count = (shift + CAP + 127) // 128
+                line = jnp.concatenate([ids[pl.ds(first + j, 1), :] for j in range(count)], axis=1)
+                names[source, :, pl.ds(0, CAP)] = line[:, shift : shift + CAP]
     grid[...] = jnp.zeros_like(grid)
-    mine.wait()
     fetch.wait()
     for k in range(BOX):
         high, low = split(held[:, k, :])
         aug_h[k] = high
         aug_l[k] = low
 
-    row = lax.broadcasted_iota(jnp.int32, (HIGH, CAP), 0)
-    column = lax.broadcasted_iota(jnp.int32, (GRID, CAP), 0)
-
-    def one_source(step, carry):
-        @pl.when(step > 0)
-        def _():
-            copy_at(step).wait()
-
-        dz, dy = offset(step)
-        source = ((z - dz + 8) % 8) * 4 + (y - dy + 4) % 4
-        name = ids[source]
-        in_row = (row == (name >> 8)).astype(F32).astype(BF)
-        in_column = (column == (name & (GRID - 1))).astype(F32).astype(BF)
-        tiles = land[source]
-        top = [tiles[2 * tile] for tile in range(FULL)] + [tiles[2 * FULL][:, :REST]]
-        bottom = [tiles[2 * tile + 1] for tile in range(FULL)] + [tiles[2 * FULL][:, REST : 2 * REST]]
-        value = jnp.concatenate([jnp.concatenate(top, axis=1), jnp.concatenate(bottom, axis=1)], axis=0)
-        both = jnp.concatenate(split(value), axis=0)
-        left = (in_row[None] * both[:, None, :]).reshape(32 * HIGH, CAP)
-        got = mm(left, in_column, NT)
-        grid[...] += (got[: 16 * HIGH] + got[16 * HIGH :]).reshape(16, HIGH, GRID)
+    row = lax.broadcasted_iota(jnp.int32, (HIGH, WIDE), 0)
+    column = lax.broadcasted_iota(jnp.int32, (GRID, WIDE), 0)
+
+    def one_pair(pair, carry):
+        lefts, rights = [], []
+        for step in (2 * pair, 2 * pair + 1):
+            @pl.when(step > 0)
+            def _():
+                copy_at(step).wait()
+
+        for step in (2 * pair, 2 * pair + 1):
+            dz, dy = offset(step)
+            name = names[((z - dz + 8) % 8) * 4 + (y - dy + 4) % 4]
+            in_row = (row == (name >> 8)).astype(F32).astype(BF)
+            in_column = (column == (name & (GRID - 1))).astype(F32).astype(BF)
+            tiles = land[step]
+            last = tiles[2 * FULL]
+            top = [tiles[2 * tile] for tile in range(FULL)] + [last]
+            bottom = [tiles[2 * tile + 1] for tile in range(FULL)] + [pltpu.roll(last, 128 - REST, 1)]
+            value = jnp.concatenate([jnp.concatenate(top, axis=1), jnp.concatenate(bottom, axis=1)], axis=0)
+            for half in split(value):
+                lefts.append((in_row[None] * half[:, None, :]).reshape(16 * HIGH, WIDE))
+                rights.append(in_column)
+        got = mm(jnp.concatenate(lefts, axis=1), jnp.concatenate(rights, axis=1), NT)
+        grid[...] += got.reshape(16, HIGH, GRID)
         return carry
 
-    lax.fori_loop(0, N_GRID, one_source, 0)
-
-
-def exchange(ids, sticks, aug):
+    lax.fori_loop(0, N_GRID // 2, one_pair, 0)
+
+
+def exchange(coeffs, high, low, ids, aug):
     return pl.pallas_call(
         exchange_kernel,
         out_shape=(
@@ -165,19 +180,22 @@
             jax.ShapeDtypeStruct((BOX, NFUNC, GRID), BF),
             jax.ShapeDtypeStruct((BOX, NFUNC, GRID), BF),
         ),
-        in_specs=[VM, ANY, ANY],
+        in_specs=[VM, VM, VM, VM, ANY],
         out_specs=(VM, VM, VM),
         scratch_shapes=[
             pltpu.VMEM((N_GRID, TILES, 8, 128), F32),
+            pltpu.VMEM((N_GRID, TILES, 8, 128), F32),
+            pltpu.VMEM((N_GRID, 1, WIDE), jnp.int32),
             pltpu.VMEM((NFUNC, BOX, GRID), F32),
-            pltpu.SemaphoreType.DMA,
+            pltpu.VMEM((CAP, 2 * KG), BF),
+            pltpu.VMEM((CAP, 2 * KG), BF),
             pltpu.SemaphoreType.DMA,
             pltpu.SemaphoreType.DMA((N_GRID,)),
             pltpu.SemaphoreType.DMA((N_GRID,)),
         ],
         compiler_params=pltpu.CompilerParams(collective_id=0, has_side_effects=True),
         name="stick_exchange",
-    )(ids, sticks, aug)
+    )(coeffs, high, low, ids, aug)
 
 
 def window_pick(y0):
@@ -464,8 +482,8 @@
 def on_device(coeffs, stick_ids, band_weights, aug_functions, atom_offsets, intersection_list, atom_slots):
     along_z, along_y, along_x = (halves(table) for table in tables())
     offsets = atom_offsets.T
-    sticks = z_transform(coeffs.reshape(2, CAP, KG), *along_z)
-    grid, aug_h, aug_l = exchange(stick_ids.reshape(N_GRID, 1, CAP), sticks, aug_functions)
+    ids = stick_ids.reshape(-1, 128)
+    grid, aug_h, aug_l = exchange(coeffs.reshape(2, CAP, KG), *along_z, ids, aug_functions)
     dens, proj = waves(offsets, band_weights, grid, *along_y, *along_x, aug_h, aug_l)
     total, shared, boxes = sums(atom_slots, band_weights, proj, dens, aug_h, aug_l)
     return final(offsets, shared, total, boxes)

time: 107 us -> 94.9 us (0.89)
  Pallas kernels: 104 us -> 93.6 us
  local copies, waits for them, and re-layouts: 1.71 us -> 0 us
    pallas_call x1 -> x0, Pallas kernels: 3.94 us -> none  [z_transform(): pl.pallas_call(z_kernel, out_shape=jax.ShapeDtypeStruct((N_GRID, TILES, 8...]
    pallas_call x1, Pallas kernels: 29.8 us -> 26.1 us  [sums(): pl.pallas_call(sum_kernel, out_shape=(jax.ShapeDtypeStruct(quarter, F32),...]
    pallas_call x1, Pallas kernels: 54.6 us -> 51.7 us  [exchange(): pl.pallas_call(exchange_kernel, out_shape=(jax.ShapeDtypeStruct((16, HIGH...]
    reshape x1 -> x0, local copies, waits for them, and re-layouts: 1.71 us -> none  [on_device(): stick_ids.reshape(N_GRID, 1, CAP)]
where the time goes in v3:
time: 94.9 us
  Pallas kernels  93.6 us (99%)
  between operations  1.29 us (1%)
    pallas_call x1, Pallas kernels, exchange(): pl.pallas_call(exchange_kernel, out_shape=(jax.ShapeDtypeStruct((16, HIGH...  51.7 us
    pallas_call x1, Pallas kernels, sums(): pl.pallas_call(sum_kernel, out_shape=(jax.ShapeDtypeStruct(quarter, F32),...  26.1 us
    pallas_call x1, Pallas kernels, waves(): pl.pallas_call(wave_kernel, out_shape=(jax.ShapeDtypeStruct((2, 4, PLANES...  13.1 us
    pallas_call x1, Pallas kernels, final(): pl.pallas_call(final_kernel, out_shape=(jax.ShapeDtypeStruct((PLANES, 32,...  2.61 us

profile of v3, /device:TPU:1, one launch (start us, length us, event | category | flops | bytes accessed | tf_op | source)
XLA Modules:
  0.0 94.9 jit_solution(17899809942326956354)
XLA Ops:
  1.3 51.7 %stick_exchange.1 = (f32[16,64,256]{2,1,0:T(8,128)}, bf16[16,128,256]{2,1,0:T(8,128)(2,1)}, bf16[16,128,256]{2,1,0:T(8,128)(2,1)}) custom-call(f32[2,688,128]{2,1,0:T(8,128)} %bitcast.3, bf16[512,256]{1,0:T(8,128)(2,1)} %constant.12.clone.table_h, bf16[512,256]{1,0:T(8,128)(2,1)} %constant.13.clone.table_l, s32[172,128]{1,0:T(8,128)} %bitcast.4, ...), custom_call_target="tpu_custom_call" | custom-call | tf_op jit(solution)/shard_map/stick_exchange/pallas_call | solution.py:176
  53.0 13.1 %waves.1 = (f32[2,4,8,32,256]{4,3,2,1,0:T(8,128)}, f32[16,128]{1,0:T(8,128)}) custom-call(s32[3,64]{1,0:T(4,128)} %bitcast.5, f32[1]{0:T(128)S(6)} %copy.14.weight, f32[16,64,256]{2,1,0:T(8,128)} %get-tuple-element.10.grid, bf16[256,512]{1,0:T(8,128)(2,1)} %constant.14.clone.yh, bf16[256,512]{1,0:T(8,128)(2,1)} %constant.15.clone.yl, ...), custom_call_target="tpu_custom_call" | custom-call | tf_op jit(solution)/shard_map/waves/pallas_call | solution.py:266
  66.1 26.1 %sums.1 = (f32[8,32,256]{2,1,0:T(8,128)}, f32[8,24,128]{2,1,0:T(8,128)}, f32[16,8,256]{2,1,0:T(8,128)}) custom-call(s32[128]{0:T(128)} %slots.1, f32[1]{0:T(128)S(6)} %copy.14.weight, f32[16,128]{1,0:T(8,128)} %get-tuple-element.13.proj, f32[2,4,8,32,256]{4,3,2,1,0:T(8,128)} %get-tuple-element.14.dens, bf16[16,128,256]{2,1,0:T(8,128)(2,1)} %get-tuple-element.11.aug_h, ...), custom_call_target="tpu_custom_call" | custom-call | tf_op jit(solution)/shard_map/sums/pallas_call | solution.py:407
  92.3 2.6 %final.1 = (f32[8,32,256]{2,1,0:T(8,128)}, f32[4,128,128]{2,1,0:T(8,128)}) custom-call(s32[3,64]{1,0:T(4,128)} %bitcast.6, f32[8,24,128]{2,1,0:T(8,128)} %get-tuple-element.15.shared, f32[8,32,256]{2,1,0:T(8,128)} %get-tuple-element.16.total, f32[16,8,256]{2,1,0:T(8,128)} %get-tuple-element.17.boxes), custom_call_target="tpu_custom_call" | custom-call | tf_op jit(solution)/shard_map/final/pallas_call | solution.py:470
